TPU v7x, 32 devices: a whole 2x2x4 slice. The times are simulated.
32 devices in a mesh: dp: 8 (over z, x), head: 4 (over y, core).
Axes of the slice: x: 2, y: 2, z: 4, core: 2. Of those that a mesh axis runs over, the one named last changes fastest.
Arguments:
- layer_input: bfloat16 [64, 197, 768], P(('dp', 'head')), may hold values from -6 to 6
- prompts: bfloat16 [100, 768], replicated, may hold values from -6 to 6
- lengths: int32 [64], P('dp'), may hold values from 1 to 100, as said below
- key_mask: int32 [64, 297], P('dp'), may hold values 0 or 1
- ln1_gain: float32 [768], replicated, may hold values from 0.1 to 1.9
- ln1_shift: float32 [768], replicated, may hold values from -1.5 to 1.5
- w_qkv: bfloat16 [3, 768, 768], P(None, 'dp', 'head'), may hold values from -0.3125 to 0.3125
- w_out: bfloat16 [768, 768], P('head', 'dp'), may hold values from -0.875 to 0.875
- b_out: float32 [768], replicated, may hold values from -1.5 to 1.5
- ln2_gain: float32 [768], replicated, may hold values from 0.1 to 1.9
- ln2_shift: float32 [768], replicated, may hold values from -1.5 to 1.5
- w_fc1: bfloat16 [768, 3072], P('dp', 'head'), may hold values from -0.21875 to 0.21875
- b_fc1: float32 [3072], P('head'), may hold values from -2.5 to 2.5
- w_fc2: bfloat16 [3072, 768], P('head', 'dp'), may hold values from -0.15625 to 0.15625
- b_fc2: float32 [768], replicated, may hold values from -1.5 to 1.5
- grad_output: bfloat16 [64, 297, 768], P(('dp', 'head')), may hold values from -6 to 6
Outputs:
- layer_output: bfloat16 [64, 297, 768], P(('dp', 'head'))
- grad_input: bfloat16 [64, 197, 768], P(('dp', 'head'))
- grad_prompts: float32 [100, 768], replicated
Inputs may be any that keep to these rules, and one draw needn't show every extreme that they name: `lengths`: each length is one of 1, 10, 50 and 100; both 1 and 100 occur.
All inputs are finite; a program needn't handle non-finite values. No bound on the sum of `key_mask` on one device may be relied on, other than what follows from the above.
Results may differ from a plain program's by a relative error of at most 0.019.
Values may be sent and summed in bfloat16 or wider, within the bound.
No kernel may reach another device: no remote copies, remote signals or barrier semaphores. Data moves between devices by JAX's collectives and lax.ppermute only.
A program may use at most 128 MiB of HBM per device.

v0:
```python
import jax
import jax.numpy as jnp
from jax import lax
from jax.sharding import PartitionSpec as P

HEAD_DIM = 64
IMG_TOK = 197
PROMPTS = 100
EPSILON = 1e-06


def layer_norm(rows, gain, shift):
    center = rows - jnp.mean(rows, axis=-1, keepdims=True)
    return (
        center * lax.rsqrt(jnp.mean(center * center, axis=-1, keepdims=True) + EPSILON) * gain
        + shift
    )


def token_masks(lengths, key_mask):
    position = lax.broadcasted_iota(jnp.int32, key_mask.shape, 1)
    used = (position < IMG_TOK) | (position - IMG_TOK < lengths[:, None])
    seen = (key_mask == 1) | (position == 0)
    return (used, used & seen)


def project(rows_b, weight):
    return jnp.einsum("isd,dc->isc", rows_b, weight, preferred_element_type=jnp.float32)


def attend(rows_b, full_qkv, visible):
    img_count, seq_len = (rows_b.shape[0], rows_b.shape[1])
    head_count = full_qkv.shape[2] // HEAD_DIM
    projected = jnp.einsum(
        "isd,tdc->tisc", rows_b, full_qkv, preferred_element_type=jnp.float32
    ).astype(jnp.bfloat16)
    projected = projected.reshape(3, img_count, seq_len, head_count, HEAD_DIM)
    query_rows, key_rows, value_rows = (projected[0], projected[1], projected[2])
    scores = jnp.einsum(
        "ishc,ithc->ihst", query_rows, key_rows, preferred_element_type=jnp.float32
    ) * HEAD_DIM ** (-0.5)
    scores = jnp.where(visible[:, None, None, :], scores, -1000000000.0)
    attn_probs = jax.nn.softmax(scores, axis=-1)
    return (query_rows, key_rows, value_rows, attn_probs)


def mix_values(probs_b, value_rows):
    img_count, seq_len = (value_rows.shape[0], value_rows.shape[1])
    context = jnp.einsum("ihst,ithc->ishc", probs_b, value_rows, preferred_element_type=jnp.float32)
    return context.astype(jnp.bfloat16).reshape(img_count, seq_len, value_rows.shape[2] * HEAD_DIM)


def mlp_back(grad_all, pre_act, fc1_rows, fc2_rows):
    grad_active_b = jnp.einsum(
        "isd,fd->isf", grad_all, fc2_rows, preferred_element_type=jnp.float32
    ).astype(jnp.bfloat16)
    _, gelu_back = jax.vjp(lambda values_in: jax.nn.gelu(values_in, approximate=False), pre_act)
    grad_pre_b = gelu_back(grad_active_b.astype(jnp.float32))[0].astype(jnp.bfloat16)
    return jnp.einsum("isf,df->isd", grad_pre_b, fc1_rows, preferred_element_type=jnp.float32)


def attn_back(grad_all, out_rows, qkv_rows, query_rows, key_rows, value_rows, attn_probs, probs_b):
    img_count, seq_len, head_count = (value_rows.shape[0], value_rows.shape[1], value_rows.shape[2])
    local_width = head_count * HEAD_DIM
    grad_context = jnp.einsum(
        "isd,cd->isc", grad_all, out_rows, preferred_element_type=jnp.float32
    ).astype(jnp.bfloat16)
    grad_context = grad_context.reshape(img_count, seq_len, head_count, HEAD_DIM)
    grad_value = jnp.einsum(
        "ihst,ishc->ithc", probs_b, grad_context, preferred_element_type=jnp.float32
    ).astype(jnp.bfloat16)
    grad_probs = jnp.einsum(
        "ishc,ithc->ihst", grad_context, value_rows, preferred_element_type=jnp.float32
    )
    grad_scores = (
        attn_probs * (grad_probs - jnp.sum(attn_probs * grad_probs, axis=-1, keepdims=True))
    ).astype(jnp.bfloat16)
    grad_query = (
        jnp.einsum("ihst,ithc->ishc", grad_scores, key_rows, preferred_element_type=jnp.float32)
        * HEAD_DIM ** (-0.5)
    ).astype(jnp.bfloat16)
    grad_key = (
        jnp.einsum("ihst,ishc->ithc", grad_scores, query_rows, preferred_element_type=jnp.float32)
        * HEAD_DIM ** (-0.5)
    ).astype(jnp.bfloat16)
    stacked = jnp.stack([grad_query, grad_key, grad_value]).reshape(
        3, img_count, seq_len, local_width
    )
    return jnp.einsum("tisc,tdc->isd", stacked, qkv_rows, preferred_element_type=jnp.float32)


def per_device(
    layer_input,
    prompts,
    lengths,
    key_mask,
    ln1_gain,
    ln1_shift,
    w_qkv,
    w_out,
    b_out,
    ln2_gain,
    ln2_shift,
    w_fc1,
    b_fc1,
    w_fc2,
    b_fc2,
    grad_output,
):
    own_count = layer_input.shape[0]
    model_width = layer_input.shape[2]
    offset = lax.axis_index("head") * own_count
    used_all, visible = token_masks(lengths, key_mask)
    used_own = lax.dynamic_slice_in_dim(used_all, offset, own_count, 0).astype(jnp.float32)[
        ..., None
    ]
    gain_one, shift_one = (ln1_gain, ln1_shift)
    gain_two, shift_two = (ln2_gain, ln2_shift)
    full_qkv, full_out, full_fc1, full_fc2 = (
        lax.all_gather(w_qkv, "dp", axis=1, tiled=True),
        lax.all_gather(w_out, "dp", axis=1, tiled=True),
        lax.all_gather(w_fc1, "dp", axis=0, tiled=True),
        lax.all_gather(w_fc2, "dp", axis=1, tiled=True),
    )
    prompt_rows = jnp.broadcast_to(
        prompts.astype(jnp.float32)[None], (own_count, PROMPTS, model_width)
    )
    stream = jnp.concatenate([layer_input.astype(jnp.float32), prompt_rows], axis=1)
    normed_attn, back_attn_norm = jax.vjp(
        lambda rows: layer_norm(rows, gain_one, shift_one), stream
    )
    normed_attn_b = normed_attn.astype(jnp.bfloat16)
    grad_rows = grad_output.astype(jnp.float32) * used_own
    gathered_attn = lax.all_gather(normed_attn_b, "head", axis=0, tiled=True)
    query_rows, key_rows, value_rows, attn_probs = attend(gathered_attn, full_qkv, visible)
    probs_b = attn_probs.astype(jnp.bfloat16)
    context = mix_values(probs_b, value_rows)
    attn_sum = lax.psum_scatter(
        project(context, full_out).astype(jnp.bfloat16), "head", scatter_dimension=0, tiled=True
    ).astype(jnp.float32)
    hidden_mid = stream + attn_sum + b_out
    normed_mlp, back_mlp_norm = jax.vjp(
        lambda rows: layer_norm(rows, gain_two, shift_two), hidden_mid
    )
    normed_mlp_b = normed_mlp.astype(jnp.bfloat16)
    gathered_mlp = lax.all_gather(normed_mlp_b, "head", axis=0, tiled=True)
    pre_act = project(gathered_mlp, full_fc1) + b_fc1
    active_b = jax.nn.gelu(pre_act, approximate=False).astype(jnp.bfloat16)
    mlp_sum = lax.psum_scatter(
        project(active_b, full_fc2).astype(jnp.bfloat16), "head", scatter_dimension=0, tiled=True
    ).astype(jnp.float32)
    result = ((hidden_mid + mlp_sum + b_fc2) * used_own).astype(jnp.bfloat16)
    held_inputs = lax.optimization_barrier((w_qkv, w_out, w_fc1, w_fc2, grad_rows))
    grad_rows = held_inputs[4]
    back_qkv, back_out, back_fc1, back_fc2 = (
        lax.all_gather(held_inputs[0], "dp", axis=1, tiled=True),
        lax.all_gather(held_inputs[1], "dp", axis=1, tiled=True),
        lax.all_gather(held_inputs[2], "dp", axis=0, tiled=True),
        lax.all_gather(held_inputs[3], "dp", axis=1, tiled=True),
    )
    grad_mlp_b = grad_rows.astype(jnp.bfloat16)
    grad_mlp_all, gathered_again = (
        lax.all_gather(grad_mlp_b, "head", axis=0, tiled=True),
        lax.all_gather(normed_mlp_b, "head", axis=0, tiled=True),
    )
    pre_act = project(gathered_again, back_fc1) + b_fc1
    grad_normed_mlp = lax.psum_scatter(
        mlp_back(grad_mlp_all, pre_act, back_fc1, back_fc2).astype(jnp.bfloat16),
        "head",
        scatter_dimension=0,
        tiled=True,
    ).astype(jnp.float32)
    grad_mid = grad_rows + back_mlp_norm(grad_normed_mlp)[0]
    grad_attn_b = grad_mid.astype(jnp.bfloat16)
    grad_attn_all, gathered_again = (
        lax.all_gather(grad_attn_b, "head", axis=0, tiled=True),
        lax.all_gather(normed_attn_b, "head", axis=0, tiled=True),
    )
    query_rows, key_rows, value_rows, attn_probs = attend(gathered_again, back_qkv, visible)
    probs_b = attn_probs.astype(jnp.bfloat16)
    grad_partial = attn_back(
        grad_attn_all, back_out, back_qkv, query_rows, key_rows, value_rows, attn_probs, probs_b
    )
    grad_normed_attn = lax.psum_scatter(
        grad_partial.astype(jnp.bfloat16), "head", scatter_dimension=0, tiled=True
    ).astype(jnp.float32)
    grad_stream = grad_mid + back_attn_norm(grad_normed_attn)[0]
    grad_input = grad_stream[:, :IMG_TOK].astype(jnp.bfloat16)
    grad_prompts = lax.psum(jnp.sum(grad_stream[:, IMG_TOK:], axis=0), ("dp", "head"))
    return (result, grad_input, grad_prompts)


def solution(mesh):
    placed = (
        P(("dp", "head"), None, None),
        P(),
        P("dp"),
        P("dp", None),
        P(),
        P(),
        P(None, "dp", "head"),
        P("head", "dp"),
        P(),
        P(),
        P(),
        P("dp", "head"),
        P("head"),
        P("head", "dp"),
        P(),
        P(("dp", "head"), None, None),
    )
    return jax.shard_map(
        per_device,
        mesh=mesh,
        in_specs=placed,
        out_specs=(P(("dp", "head"), None, None), P(("dp", "head"), None, None), P()),
        check_vma=False,
    )
```

profile of v0, /device:TPU:8, one launch (start us, length us, event | category | flops | bytes accessed | tf_op | source)
XLA Modules:
  0.0 717.3 jit_solution(3644398181313778874)
XLA Ops:
  12.6 36.7 %all_gather.39 = bf16[3,768,192]{2,0,1:T(4,128)(2,1)} all-gather(bf16[3,96,192]{2,0,1:T(4,128)(2,1)S(1)} %copy.34), channel_id=1, replica_groups=mesh['dp'=8,'head'=4] {'dp'}, dimensions={1}, use_global_device_ids=true | all-gather | bytes 995328 | tf_op jit(solution)/shard_map/all_gather | solution.py:120
  52.7 30.5 %all_gather.40 = bf16[192,768]{0,1:T(8,128)(2,1)S(1)} all-gather(bf16[192,96]{0,1:T(8,128)(2,1)S(1)} %copy.37), channel_id=1, replica_groups=mesh['dp'=8,'head'=4] {'dp'}, dimensions={1}, use_global_device_ids=true | all-gather | bytes 331776 | tf_op jit(solution)/shard_map/all_gather | solution.py:121
  90.5 8.2 %fusion.168 = (f32[8,3,297]{2,1,0:T(4,128)S(1)}, f32[8,3,297,297]{2,3,1,0:T(8,128)}) fusion(pred[8,297]{1,0:T(8,128)(4,1)S(1)} %get-tuple-element.30, bf16[8,297,3,64]{1,3,2,0:T(8,128)(2,1)} %bitcast.105, bf16[8,297,3,64]{1,3,2,0:T(8,128)(2,1)} %bitcast.104), kind=kOutput, calls=%fused_computation.222 | convolution fusion | flops 279446432 | bytes 10323720 | tf_op jit(solution)/shard_map/sub | solution.py:43
  98.7 5.8 fusion.73
  110.4 41.4 %reduce-scatter.5.cloned.1.call-done = bf16[2,297,768]{2,1,0:T(8,128)(2,1)} async-done(((bf16[8,297,768]{2,1,0:T(8,128)(2,1)}), bf16[2,297,768]{2,1,0:T(8,128)(2,1)}) %reduce-scatter.5.cloned.1.call-update) | async-done | bytes 912400 | tf_op jit(solution)/shard_map/reduce_scatter | solution.py:138
  161.7 26.8 %all-gather.11.cloned.1.call-done = bf16[8,297,768]{2,1,0:T(8,128)(2,1)} async-done(((bf16[2,297,768]{2,1,0:T(8,128)(2,1)}), bf16[8,297,768]{2,1,0:T(8,128)(2,1)}) %all-gather.11.cloned.1.call-update) | async-done | bytes 3649552 | tf_op jit(solution)/shard_map/all_gather | solution.py:146
  188.5 8.4 %fusion.82 = f32[8,297,768]{2,1,0:T(8,128)} fusion(bf16[8,297,768]{2,1,0:T(8,128)(2,1)} %all-gather.11.cloned.1.call-done, bf16[768,768]{1,0:T(8,128)(2,1)} %all-gather.17.cloned.1.call-done), kind=kOutput, calls=%fused_computation.120 | convolution fusion | flops 2802843648 | bytes 12128256 | tf_op jit(solution)/shard_map/isd,dc->isc/dot_general | solution.py:28
  196.9 34.4 %all-gather.21.cloned.1.call-done = bf16[768,768]{0,1:T(8,128)(2,1)} async-done(((bf16[768,96]{0,1:T(8,128)(2,1)}), bf16[768,768]{0,1:T(8,128)(2,1)}) %all-gather.21.cloned.1.call-update) | async-done | bytes 1179664 | tf_op jit(solution)/shard_map/all_gather | solution.py:159
  231.3 32.9 %all-gather.19.cloned.1.call-done = bf16[8,297,768]{2,1,0:T(8,128)(2,1)} async-done(((bf16[2,297,768]{2,1,0:T(8,128)(2,1)}), bf16[8,297,768]{2,1,0:T(8,128)(2,1)}) %all-gather.19.cloned.1.call-update) | async-done | bytes 3649552 | tf_op jit(solution)/shard_map/all_gather | solution.py:163
  264.2 27.0 %fusion.57 = bf16[8,297,768]{2,1,0:T(8,128)(2,1)} fusion(f32[8,297,768]{2,1,0:T(8,128)} %fusion.82, f32[768]{0:T(1024)S(1)} %copy-done.35, bf16[8,297,768]{2,1,0:T(8,128)(2,1)} %all-gather.19.cloned.1.call-done, bf16[768,768]{0,1:T(8,128)(2,1)} %all-gather.21.cloned.1.call-done, bf16[768,768]{1,0:T(8,128)(2,1)} %all-gather.17.cloned.1.call-done), kind=kOutput, calls=%fused_computation.89 | convolution fusion | flops 5744369664 | bytes 16960512 | tf_op jit(solution)/shard_map/isf,df->isd/dot_general | solution.py:59
  291.2 9.2 %reduce-scatter.7.cloned.1.call-start = ((), (), s32[]{:S(2)}) async-start(), calls=%async_computation.9 | async-start | bytes 4669440 | tf_op jit(solution)/shard_map/reduce_scatter | solution.py:149
  300.4 6.6 all-gather.13.cloned.1.call-done
  307.0 10.3 %fusion.70 = (u8[297,768]{1,0:T(8,128)(4,1)S(1)}, u8[297,768]{1,0:T(8,128)(4,1)S(1)}, f32[8,297,768]{2,1,0:T(8,128)}) fusion(f32[768]{0:T(1024)S(1)} %copy-done.35, bf16[8,297,768]{2,1,0:T(8,128)(2,1)} %all-gather.11.cloned.1.call-done, bf16[768,768]{1,0:T(8,128)(2,1)} %all-gather.13.cloned.1.call-done), kind=kOutput, calls=%fused_computation.109 | convolution fusion | flops 2827934208 | bytes 12587520 | tf_op jit(solution)/shard_map/isd,dc->isc/dot_general | solution.py:28
  317.2 32.0 %all-gather.15.cloned.1.call-done = bf16[768,768]{0,1:T(8,128)(2,1)} async-done(((bf16[768,96]{0,1:T(8,128)(2,1)}), bf16[768,768]{0,1:T(8,128)(2,1)}) %all-gather.15.cloned.1.call-update) | async-done | bytes 1179664 | tf_op jit(solution)/shard_map/all_gather | solution.py:123
  349.3 23.0 %fusion.60 = bf16[8,297,768]{2,1,0:T(8,128)(2,1)} fusion(f32[8,297,768]{2,1,0:T(8,128)} %get-tuple-element.33, f32[768]{0:T(1024)S(1)} %copy-done.35, bf16[768,768]{0,1:T(8,128)(2,1)} %all-gather.15.cloned.1.call-done, u8[297,768]{1,0:T(8,128)(4,1)S(1)} %get-tuple-element.20, u8[297,768]{1,0:T(8,128)(4,1)S(1)} %get-tuple-element.19), kind=kOutput, calls=%fused_computation.90 | convolution fusion | flops 2934226944 | bytes 12587520 | tf_op jit(solution)/shard_map/isd,dc->isc/dot_general | solution.py:28
  375.4 38.2 %reduce-scatter.7.cloned.1.call-done = bf16[2,297,768]{2,1,0:T(8,128)(2,1)} async-done(((bf16[8,297,768]{2,1,0:T(8,128)(2,1)}), bf16[2,297,768]{2,1,0:T(8,128)(2,1)}) %reduce-scatter.7.cloned.1.call-update) | async-done | bytes 912400 | tf_op jit(solution)/shard_map/reduce_scatter | solution.py:149
  417.5 28.5 %all_gather.49 = bf16[192,768]{0,1:T(8,128)(2,1)S(1)} all-gather(bf16[192,96]{0,1:T(8,128)(2,1)S(1)} %copy.42), channel_id=1, replica_groups=mesh['dp'=8,'head'=4] {'dp'}, dimensions={1}, use_global_device_ids=true | all-gather | bytes 331776 | tf_op jit(solution)/shard_map/all_gather | solution.py:157
  446.1 39.4 %all_gather.47 = bf16[3,768,192]{2,0,1:T(4,128)(2,1)S(1)} all-gather(bf16[3,96,192]{2,0,1:T(4,128)(2,1)S(1)} %copy.40), channel_id=1, replica_groups=mesh['dp'=8,'head'=4] {'dp'}, dimensions={1}, use_global_device_ids=true | all-gather | bytes 995328 | tf_op jit(solution)/shard_map/all_gather | solution.py:156
  485.5 7.7 %convert_bitcast_fusion = bf16[3,8,297,192]{2,3,1,0:T(8,128)(2,1)S(1)} fusion(bf16[8,297,768]{2,1,0:T(8,128)(2,1)} %all-gather.9.cloned.1.call-done, bf16[3,768,192,1]{2,0,1,3:T(4,128)(2,1)S(1)} %bitcast.101), kind=kOutput, calls=%fused_computation.84 | convolution fusion | flops 2103501312 | bytes 7271424 | tf_op jit(solution)/shard_map/isd,tdc->tisc/dot_general | solution.py:34
  495.2 8.2 %fusion.169 = (f32[8,3,297]{2,1,0:T(4,128)S(1)}, f32[8,3,297,297]{2,3,1,0:T(8,128)}) fusion(pred[8,297]{1,0:T(8,128)(4,1)S(1)} %copy-done.33, bf16[8,297,3,64]{1,3,2,0:T(8,128)(2,1)} %bitcast.98, bf16[8,297,3,64]{1,3,2,0:T(8,128)(2,1)} %bitcast.96), kind=kOutput, calls=%fused_computation.223 | convolution fusion | flops 279446432 | bytes 10323720 | tf_op jit(solution)/shard_map/sub | solution.py:43
  507.1 7.6 %fusion.74 = bf16[8,3,64,297]{3,2,1,0:T(8,128)(2,1)} fusion(bf16[8,297,3,64]{1,3,2,0:T(8,128)(2,1)S(1)} %bitcast.109, f32[8,3,297,297]{2,3,1,0:T(8,128)} %get-tuple-element.35, f32[8,3,297]{2,1,0:T(4,128)S(1)} %get-tuple-element.34), kind=kOutput, calls=%fused_computation.113 | convolution fusion | flops 275668288 | bytes 10321344 | tf_op jit(solution)/shard_map/ihst,ishc->ithc/dot_general | solution.py:69
  525.0 5.4 bitcast_convert_fusion
  530.5 42.3 %reduce-scatter.11.cloned.1.call-done = bf16[2,297,768]{2,1,0:T(8,128)(2,1)} async-done(((bf16[8,297,768]{2,1,0:T(8,128)(2,1)}), bf16[2,297,768]{2,1,0:T(8,128)(2,1)}) %reduce-scatter.11.cloned.1.call-update) | async-done | bytes 912400 | tf_op jit(solution)/shard_map/reduce_scatter | solution.py:184
  585.8 122.2 %all-reduce.2.cloned.1.call-done = f32[100,768]{1,0:T(8,128)} async-done(((f32[100,768]{1,0:T(8,128)}), f32[100,768]{1,0:T(8,128)}) %all-reduce.2.cloned.1.call-update) | async-done | bytes 307216 | tf_op jit(solution)/shard_map/psum | solution.py:189
  (159 shorter events, 68.2 us)
Async XLA Ops:
  8.0 75.3 %all-gather.9.cloned.1.call-start = ((), (), s32[]{:S(2)}) async-start(), calls=%async_computation.4 | async-start | bytes 4669440 | tf_op jit(solution)/shard_map/all_gather | solution.py:134
  12.2 71.0 %copy-start.28 = (s32[8,297]{1,0:T(8,128)S(1)}, s32[8,297]{1,0:T(8,128)}, u32[]{:S(2)}) copy-start(s32[8,297]{1,0:T(8,128)} %param.19) | copy-start | bytes 28516
  12.2 71.0 %copy-start.34 = (s32[8]{0:T(128)S(1)}, s32[8]{0:T(128)}, u32[]{:S(2)}) copy-start(s32[8]{0:T(128)} %param.18) | copy-start | bytes 100
  12.2 139.5 %reduce-scatter.5.cloned.1.call-start = ((), (), s32[]{:S(2)}) async-start(), calls=%async_computation.5 | async-start | bytes 4669440 | tf_op jit(solution)/shard_map/reduce_scatter | solution.py:138
  107.7 44.1 %copy-start.12 = (f32[768]{0:T(1024)S(1)}, f32[768]{0:T(1024)}, u32[]{:S(2)}) copy-start(f32[768]{0:T(1024)} %param.24) | copy-start | bytes 9220
  107.7 54.0 %all-gather.17.cloned.1.call-start = ((), (), s32[]{:S(2)}) async-start(), calls=%async_computation.10 | async-start | bytes 1327104 | tf_op jit(solution)/shard_map/all_gather | solution.py:158
  110.3 44.8 %copy-start.17 = (f32[768]{0:T(1024)S(1)}, f32[768]{0:T(1024)}, u32[]{:S(2)}) copy-start(f32[768]{0:T(1024)} %param.25) | copy-start | bytes 9220
  110.3 44.8 %copy-start.30 = (f32[768]{0:T(1024)S(1)}, f32[768]{0:T(1024)}, u32[]{:S(2)}) copy-start(f32[768]{0:T(1024)} %param.26) | copy-start | bytes 9220
  110.3 78.1 %all-gather.11.cloned.1.call-start = ((), (), s32[]{:S(2)}) async-start(), calls=%async_computation.6 | async-start | bytes 4669440 | tf_op jit(solution)/shard_map/all_gather | solution.py:146
  156.6 74.7 %all-gather.21.cloned.1.call-start = ((), (), s32[]{:S(2)}) async-start(), calls=%async_computation.12 | async-start | bytes 1327104 | tf_op jit(solution)/shard_map/all_gather | solution.py:159
  157.2 107.0 %all-gather.19.cloned.1.call-start = ((), (), s32[]{:S(2)}) async-start(), calls=%async_computation.11 | async-start | bytes 4669440 | tf_op jit(solution)/shard_map/all_gather | solution.py:163
  159.9 147.1 %all-gather.13.cloned.1.call-start = ((), (), s32[]{:S(2)}) async-start(), calls=%async_computation.7 | async-start | bytes 1327104 | tf_op jit(solution)/shard_map/all_gather | solution.py:122
  160.6 188.6 %all-gather.15.cloned.1.call-start = ((), (), s32[]{:S(2)}) async-start(), calls=%async_computation.8 | async-start | bytes 1327104 | tf_op jit(solution)/shard_map/all_gather | solution.py:123
  161.4 102.9 %copy-start.35 = (f32[768]{0:T(1024)S(1)}, f32[768]{0:T(1024)}, u32[]{:S(2)}) copy-start(f32[768]{0:T(1024)} %param.28) | copy-start | bytes 9220
  161.4 211.0 %reduce-scatter.9.cloned.1.call-start = ((), (), s32[]{:S(2)}) async-start(), calls=%async_computation.13 | async-start | bytes 4669440 | tf_op jit(solution)/shard_map/reduce_scatter | solution.py:167
  291.2 122.4 %reduce-scatter.7.cloned.1.call-start = ((), (), s32[]{:S(2)}) async-start(), calls=%async_computation.9 | async-start | bytes 4669440 | tf_op jit(solution)/shard_map/reduce_scatter | solution.py:149
  372.3 131.1 %all-gather.23.cloned.1.call-start = ((), (), s32[]{:S(2)}) async-start(), calls=%async_computation.14 | async-start | bytes 4669440 | tf_op jit(solution)/shard_map/all_gather | solution.py:176
  375.4 42.0 %copy-start.11 = (bf16[3,96,192]{2,1,0:T(8,128)(2,1)S(1)}, bf16[3,96,192]{2,1,0:T(8,128)(2,1)}, u32[]{:S(2)}) copy-start(bf16[3,96,192]{2,1,0:T(8,128)(2,1)} %param.22) | copy-start | bytes 331780
  417.2 155.5 %reduce-scatter.11.cloned.1.call-start = ((), (), s32[]{:S(2)}) async-start(), calls=%async_computation.15 | async-start | bytes 4669440 | tf_op jit(solution)/shard_map/reduce_scatter | solution.py:184
  530.4 42.4 %copy-start.16 = (f32[2,297]{1,0:T(2,128)S(1)}, f32[2,297]{1,0:T(2,128)}, u32[]{:S(2)}) copy-start(f32[2,297]{1,0:T(2,128)} %copy-done.15) | copy-start | bytes 7132
  530.4 42.4 %copy-start.19 = (f32[768]{0:T(1024)S(1)}, f32[768]{0:T(1024)}, u32[]{:S(2)}) copy-start(f32[768]{0:T(1024)} %param.20) | copy-start | bytes 9220
  530.4 44.2 %copy-start.25 = (f32[2,297]{1,0:T(2,128)S(1)}, f32[2,297]{1,0:T(2,128)}, u32[]{:S(2)}) copy-start(f32[2,297]{1,0:T(2,128)} %copy-done.24) | copy-start | bytes 7132
  530.4 44.2 %copy-start.21 = (f32[2,297]{1,0:T(2,128)S(1)}, f32[2,297]{1,0:T(2,128)}, u32[]{:S(2)}) copy-start(f32[2,297]{1,0:T(2,128)} %copy-done.20) | copy-start | bytes 7132
  530.4 177.6 %all-reduce.2.cloned.1.call-start = ((), (), s32[]{:S(2)}) async-start(), calls=%async_computation.16 | async-start | bytes 638976 | tf_op jit(solution)/shard_map/psum | solution.py:189
  (30 other events, 224.9 us)
Sparse Core Ops, SparseCore 0:
  12.4 33.0 all-gather.8
  107.8 43.8 reduce-scatter.4
  291.3 41.6 reduce-scatter.8
  372.4 41.1 reduce-scatter.6
  580.5 127.5 all-reduce.1
Sparse Core Ops, SparseCore 1:
  110.6 42.7 all-gather.16
  156.7 31.7 all-gather.10
  190.8 40.5 all-gather.20
  233.0 31.2 all-gather.18
  266.4 40.5 all-gather.12
  309.2 40.0 all-gather.14
  417.3 31.7 all-gather.22
  530.5 42.2 reduce-scatter.10
where the time goes:
time: 726 us; the launch traced here: 717 us
  waiting for transfers between devices  379 us (52%)
  blocking collectives  135 us (19%)
  matrix products  132 us (18%)
  other arithmetic  26.4 us (4%)
  local copies, waits for them, and re-layouts  18.9 us (3%)
  between operations  16.4 us (2%)
  starting transfers between devices  9.95 us (1%)
    psum x1, waiting for transfers between devices, per_device(): lax.psum(jnp.sum(grad_stream[:, IMG_TOK:], axis=0), ('dp', 'head'))  122 us
    dot_general x4, matrix products, project(): jnp.einsum('isd,dc->isc', rows_b, weight, preferred_element_type=jnp.floa...  44.9 us
    reduce_scatter x1, waiting for transfers between devices, per_device(): lax.psum_scatter(grad_partial.astype(jnp.bfloat16), 'head', scatter_dimen...  42.3 us
    reduce_scatter x1, waiting for transfers between devices, per_device(): lax.psum_scatter(project(context, full_out).astype(jnp.bfloat16), 'head',...  41.4 us
    all_gather x1, blocking collectives, per_device(): lax.all_gather(held_inputs[0], 'dp', axis=1, tiled=True)  39.4 us
    reduce_scatter x1, waiting for transfers between devices, per_device(): lax.psum_scatter(project(active_b, full_fc2).astype(jnp.bfloat16), 'head'...  38.2 us
    all_gather x1, blocking collectives, per_device(): lax.all_gather(w_qkv, 'dp', axis=1, tiled=True)  36.7 us
    all_gather x1, waiting for transfers between devices, per_device(): lax.all_gather(held_inputs[3], 'dp', axis=1, tiled=True)  34.4 us
  transfers between devices with their start and end apart: 13, of which 9 were waited for; matrix products, arithmetic and copies ran while one was open for 15% of the time, Pallas kernels for 0%

commit v1 on v0

--- a/solution.py
+++ b/solution.py
@@ -186,7 +186,7 @@
     ).astype(jnp.float32)
     grad_stream = grad_mid + back_attn_norm(grad_normed_attn)[0]
     grad_input = grad_stream[:, :IMG_TOK].astype(jnp.bfloat16)
-    grad_prompts = lax.psum(jnp.sum(grad_stream[:, IMG_TOK:], axis=0), ("dp", "head"))
+    grad_prompts = lax.psum(lax.psum(jnp.sum(grad_stream[:, IMG_TOK:], axis=0), "head"), "dp")
     return (result, grad_input, grad_prompts)
 
 

time: 726 us -> 703 us (0.968)
  waiting for transfers between devices: 379 us -> 354 us
    psum x1 -> x2, waiting for transfers between devices: 122 us -> 97.1 us  [the longest x1 64.9 us: per_device(): lax.psum(lax.psum(jnp.sum(grad_stream[:, IMG_TOK:], axis=0), 'head'), 'dp')]
  transfers between devices with their start and end apart: 13 -> 14, of which waited for: 9 -> 10; matrix products, arithmetic and copies ran while one was open for 15% -> 16% of each run, Pallas kernels for 0% -> 0%
where the time goes in v1:
time: 703 us; the launch traced here: 692 us
  waiting for transfers between devices  354 us (50%)
  blocking collectives  135 us (19%)
  matrix products  132 us (19%)
  other arithmetic  26.4 us (4%)
  local copies, waits for them, and re-layouts  18.9 us (3%)
  between operations  16.6 us (2%)
  starting transfers between devices  10 us (1%)
    psum x1, waiting for transfers between devices, per_device(): lax.psum(lax.psum(jnp.sum(grad_stream[:, IMG_TOK:], axis=0), 'head'), 'dp')  64.9 us
    dot_general x4, matrix products, project(): jnp.einsum('isd,dc->isc', rows_b, weight, preferred_element_type=jnp.floa...  44.9 us
    reduce_scatter x1, waiting for transfers between devices, per_device(): lax.psum_scatter(grad_partial.astype(jnp.bfloat16), 'head', scatter_dimen...  42.3 us
    reduce_scatter x1, waiting for transfers between devices, per_device(): lax.psum_scatter(project(context, full_out).astype(jnp.bfloat16), 'head',...  41.4 us
    all_gather x1, blocking collectives, per_device(): lax.all_gather(held_inputs[0], 'dp', axis=1, tiled=True)  39.4 us
    reduce_scatter x1, waiting for transfers between devices, per_device(): lax.psum_scatter(project(active_b, full_fc2).astype(jnp.bfloat16), 'head'...  38.2 us
    all_gather x1, blocking collectives, per_device(): lax.all_gather(w_qkv, 'dp', axis=1, tiled=True)  36.7 us
    all_gather x1, waiting for transfers between devices, per_device(): lax.all_gather(held_inputs[3], 'dp', axis=1, tiled=True)  34.4 us
  transfers between devices with their start and end apart: 14, of which 10 were waited for; matrix products, arithmetic and copies ran while one was open for 16% of the time, Pallas kernels for 0%

profile of v1, /device:TPU:8, one launch (start us, length us, event | category | flops | bytes accessed | tf_op | source)
XLA Modules:
  0.0 692.5 jit_solution(13497543393800033907)
XLA Ops:
  12.6 36.7 %all_gather.39 = bf16[3,768,192]{2,0,1:T(4,128)(2,1)} all-gather(bf16[3,96,192]{2,0,1:T(4,128)(2,1)S(1)} %copy.34), channel_id=1, replica_groups=mesh['dp'=8,'head'=4] {'dp'}, dimensions={1}, use_global_device_ids=true | all-gather | bytes 995328 | tf_op jit(solution)/shard_map/all_gather | solution.py:120
  52.7 30.5 %all_gather.40 = bf16[192,768]{0,1:T(8,128)(2,1)S(1)} all-gather(bf16[192,96]{0,1:T(8,128)(2,1)S(1)} %copy.37), channel_id=1, replica_groups=mesh['dp'=8,'head'=4] {'dp'}, dimensions={1}, use_global_device_ids=true | all-gather | bytes 331776 | tf_op jit(solution)/shard_map/all_gather | solution.py:121
  90.5 8.2 %fusion.168 = (f32[8,3,297]{2,1,0:T(4,128)S(1)}, f32[8,3,297,297]{2,3,1,0:T(8,128)}) fusion(pred[8,297]{1,0:T(8,128)(4,1)S(1)} %get-tuple-element.30, bf16[8,297,3,64]{1,3,2,0:T(8,128)(2,1)} %bitcast.105, bf16[8,297,3,64]{1,3,2,0:T(8,128)(2,1)} %bitcast.104), kind=kOutput, calls=%fused_computation.222 | convolution fusion | flops 279446432 | bytes 10323720 | tf_op jit(solution)/shard_map/sub | solution.py:43
  98.7 5.8 fusion.73
  110.4 41.4 %reduce-scatter.5.cloned.1.call-done = bf16[2,297,768]{2,1,0:T(8,128)(2,1)} async-done(((bf16[8,297,768]{2,1,0:T(8,128)(2,1)}), bf16[2,297,768]{2,1,0:T(8,128)(2,1)}) %reduce-scatter.5.cloned.1.call-update) | async-done | bytes 912400 | tf_op jit(solution)/shard_map/reduce_scatter | solution.py:138
  161.7 26.8 %all-gather.11.cloned.1.call-done = bf16[8,297,768]{2,1,0:T(8,128)(2,1)} async-done(((bf16[2,297,768]{2,1,0:T(8,128)(2,1)}), bf16[8,297,768]{2,1,0:T(8,128)(2,1)}) %all-gather.11.cloned.1.call-update) | async-done | bytes 3649552 | tf_op jit(solution)/shard_map/all_gather | solution.py:146
  188.5 8.4 %fusion.82 = f32[8,297,768]{2,1,0:T(8,128)} fusion(bf16[8,297,768]{2,1,0:T(8,128)(2,1)} %all-gather.11.cloned.1.call-done, bf16[768,768]{1,0:T(8,128)(2,1)} %all-gather.17.cloned.1.call-done), kind=kOutput, calls=%fused_computation.120 | convolution fusion | flops 2802843648 | bytes 12128256 | tf_op jit(solution)/shard_map/isd,dc->isc/dot_general | solution.py:28
  196.9 34.4 %all-gather.21.cloned.1.call-done = bf16[768,768]{0,1:T(8,128)(2,1)} async-done(((bf16[768,96]{0,1:T(8,128)(2,1)}), bf16[768,768]{0,1:T(8,128)(2,1)}) %all-gather.21.cloned.1.call-update) | async-done | bytes 1179664 | tf_op jit(solution)/shard_map/all_gather | solution.py:159
  231.3 32.9 %all-gather.19.cloned.1.call-done = bf16[8,297,768]{2,1,0:T(8,128)(2,1)} async-done(((bf16[2,297,768]{2,1,0:T(8,128)(2,1)}), bf16[8,297,768]{2,1,0:T(8,128)(2,1)}) %all-gather.19.cloned.1.call-update) | async-done | bytes 3649552 | tf_op jit(solution)/shard_map/all_gather | solution.py:163
  264.2 27.0 %fusion.57 = bf16[8,297,768]{2,1,0:T(8,128)(2,1)} fusion(f32[8,297,768]{2,1,0:T(8,128)} %fusion.82, f32[768]{0:T(1024)S(1)} %copy-done.35, bf16[8,297,768]{2,1,0:T(8,128)(2,1)} %all-gather.19.cloned.1.call-done, bf16[768,768]{0,1:T(8,128)(2,1)} %all-gather.21.cloned.1.call-done, bf16[768,768]{1,0:T(8,128)(2,1)} %all-gather.17.cloned.1.call-done), kind=kOutput, calls=%fused_computation.89 | convolution fusion | flops 5744369664 | bytes 16960512 | tf_op jit(solution)/shard_map/isf,df->isd/dot_general | solution.py:59
  291.2 9.2 %reduce-scatter.7.cloned.1.call-start = ((), (), s32[]{:S(2)}) async-start(), calls=%async_computation.9 | async-start | bytes 4669440 | tf_op jit(solution)/shard_map/reduce_scatter | solution.py:149
  300.4 6.6 all-gather.13.cloned.1.call-done
  307.0 10.3 %fusion.70 = (u8[297,768]{1,0:T(8,128)(4,1)S(1)}, u8[297,768]{1,0:T(8,128)(4,1)S(1)}, f32[8,297,768]{2,1,0:T(8,128)}) fusion(f32[768]{0:T(1024)S(1)} %copy-done.35, bf16[8,297,768]{2,1,0:T(8,128)(2,1)} %all-gather.11.cloned.1.call-done, bf16[768,768]{1,0:T(8,128)(2,1)} %all-gather.13.cloned.1.call-done), kind=kOutput, calls=%fused_computation.109 | convolution fusion | flops 2827934208 | bytes 12587520 | tf_op jit(solution)/shard_map/isd,dc->isc/dot_general | solution.py:28
  317.2 32.0 %all-gather.15.cloned.1.call-done = bf16[768,768]{0,1:T(8,128)(2,1)} async-done(((bf16[768,96]{0,1:T(8,128)(2,1)}), bf16[768,768]{0,1:T(8,128)(2,1)}) %all-gather.15.cloned.1.call-update) | async-done | bytes 1179664 | tf_op jit(solution)/shard_map/all_gather | solution.py:123
  349.3 23.0 %fusion.60 = bf16[8,297,768]{2,1,0:T(8,128)(2,1)} fusion(f32[8,297,768]{2,1,0:T(8,128)} %get-tuple-element.33, f32[768]{0:T(1024)S(1)} %copy-done.35, bf16[768,768]{0,1:T(8,128)(2,1)} %all-gather.15.cloned.1.call-done, u8[297,768]{1,0:T(8,128)(4,1)S(1)} %get-tuple-element.20, u8[297,768]{1,0:T(8,128)(4,1)S(1)} %get-tuple-element.19), kind=kOutput, calls=%fused_computation.90 | convolution fusion | flops 2934226944 | bytes 12587520 | tf_op jit(solution)/shard_map/isd,dc->isc/dot_general | solution.py:28
  375.4 38.2 %reduce-scatter.7.cloned.1.call-done = bf16[2,297,768]{2,1,0:T(8,128)(2,1)} async-done(((bf16[8,297,768]{2,1,0:T(8,128)(2,1)}), bf16[2,297,768]{2,1,0:T(8,128)(2,1)}) %reduce-scatter.7.cloned.1.call-update) | async-done | bytes 912400 | tf_op jit(solution)/shard_map/reduce_scatter | solution.py:149
  417.5 28.5 %all_gather.49 = bf16[192,768]{0,1:T(8,128)(2,1)S(1)} all-gather(bf16[192,96]{0,1:T(8,128)(2,1)S(1)} %copy.42), channel_id=1, replica_groups=mesh['dp'=8,'head'=4] {'dp'}, dimensions={1}, use_global_device_ids=true | all-gather | bytes 331776 | tf_op jit(solution)/shard_map/all_gather | solution.py:157
  446.1 39.4 %all_gather.47 = bf16[3,768,192]{2,0,1:T(4,128)(2,1)S(1)} all-gather(bf16[3,96,192]{2,0,1:T(4,128)(2,1)S(1)} %copy.40), channel_id=1, replica_groups=mesh['dp'=8,'head'=4] {'dp'}, dimensions={1}, use_global_device_ids=true | all-gather | bytes 995328 | tf_op jit(solution)/shard_map/all_gather | solution.py:156
  485.5 7.7 %convert_bitcast_fusion = bf16[3,8,297,192]{2,3,1,0:T(8,128)(2,1)S(1)} fusion(bf16[8,297,768]{2,1,0:T(8,128)(2,1)} %all-gather.9.cloned.1.call-done, bf16[3,768,192,1]{2,0,1,3:T(4,128)(2,1)S(1)} %bitcast.101), kind=kOutput, calls=%fused_computation.84 | convolution fusion | flops 2103501312 | bytes 7271424 | tf_op jit(solution)/shard_map/isd,tdc->tisc/dot_general | solution.py:34
  495.2 8.2 %fusion.169 = (f32[8,3,297]{2,1,0:T(4,128)S(1)}, f32[8,3,297,297]{2,3,1,0:T(8,128)}) fusion(pred[8,297]{1,0:T(8,128)(4,1)S(1)} %copy-done.33, bf16[8,297,3,64]{1,3,2,0:T(8,128)(2,1)} %bitcast.98, bf16[8,297,3,64]{1,3,2,0:T(8,128)(2,1)} %bitcast.96), kind=kOutput, calls=%fused_computation.223 | convolution fusion | flops 279446432 | bytes 10323720 | tf_op jit(solution)/shard_map/sub | solution.py:43
  507.1 7.6 %fusion.74 = bf16[8,3,64,297]{3,2,1,0:T(8,128)(2,1)} fusion(bf16[8,297,3,64]{1,3,2,0:T(8,128)(2,1)S(1)} %bitcast.109, f32[8,3,297,297]{2,3,1,0:T(8,128)} %get-tuple-element.35, f32[8,3,297]{2,1,0:T(4,128)S(1)} %get-tuple-element.34), kind=kOutput, calls=%fused_computation.113 | convolution fusion | flops 275668288 | bytes 10321344 | tf_op jit(solution)/shard_map/ihst,ishc->ithc/dot_general | solution.py:69
  530.5 42.3 %reduce-scatter.11.cloned.1.call-done = bf16[2,297,768]{2,1,0:T(8,128)(2,1)} async-done(((bf16[8,297,768]{2,1,0:T(8,128)(2,1)}), bf16[2,297,768]{2,1,0:T(8,128)(2,1)}) %reduce-scatter.11.cloned.1.call-update) | async-done | bytes 912400 | tf_op jit(solution)/shard_map/reduce_scatter | solution.py:184
  580.4 32.2 %all-reduce.3.cloned.1.call-done = f32[100,768]{1,0:T(8,128)} async-done(((f32[100,768]{1,0:T(8,128)}), f32[100,768]{1,0:T(8,128)}) %all-reduce.3.cloned.1.call-update) | async-done | bytes 307216 | tf_op jit(solution)/shard_map/psum | solution.py:189
  618.1 64.9 %all-reduce.5.cloned.1.call-done = f32[100,768]{1,0:T(8,128)} async-done(((f32[100,768]{1,0:T(8,128)}), f32[100,768]{1,0:T(8,128)}) %all-reduce.5.cloned.1.call-update) | async-done | bytes 307216 | tf_op jit(solution)/shard_map/psum | solution.py:189
  (162 shorter events, 73.7 us)
Async XLA Ops:
  8.0 75.3 %all-gather.9.cloned.1.call-start = ((), (), s32[]{:S(2)}) async-start(), calls=%async_computation.4 | async-start | bytes 4669440 | tf_op jit(solution)/shard_map/all_gather | solution.py:134
  12.2 71.0 %copy-start.28 = (s32[8,297]{1,0:T(8,128)S(1)}, s32[8,297]{1,0:T(8,128)}, u32[]{:S(2)}) copy-start(s32[8,297]{1,0:T(8,128)} %param.19) | copy-start | bytes 28516
  12.2 71.0 %copy-start.34 = (s32[8]{0:T(128)S(1)}, s32[8]{0:T(128)}, u32[]{:S(2)}) copy-start(s32[8]{0:T(128)} %param.18) | copy-start | bytes 100
  12.2 139.5 %reduce-scatter.5.cloned.1.call-start = ((), (), s32[]{:S(2)}) async-start(), calls=%async_computation.5 | async-start | bytes 4669440 | tf_op jit(solution)/shard_map/reduce_scatter | solution.py:138
  107.7 44.1 %copy-start.12 = (f32[768]{0:T(1024)S(1)}, f32[768]{0:T(1024)}, u32[]{:S(2)}) copy-start(f32[768]{0:T(1024)} %param.24) | copy-start | bytes 9220
  107.7 54.0 %all-gather.17.cloned.1.call-start = ((), (), s32[]{:S(2)}) async-start(), calls=%async_computation.10 | async-start | bytes 1327104 | tf_op jit(solution)/shard_map/all_gather | solution.py:158
  110.3 44.8 %copy-start.17 = (f32[768]{0:T(1024)S(1)}, f32[768]{0:T(1024)}, u32[]{:S(2)}) copy-start(f32[768]{0:T(1024)} %param.25) | copy-start | bytes 9220
  110.3 44.8 %copy-start.30 = (f32[768]{0:T(1024)S(1)}, f32[768]{0:T(1024)}, u32[]{:S(2)}) copy-start(f32[768]{0:T(1024)} %param.26) | copy-start | bytes 9220
  110.3 78.1 %all-gather.11.cloned.1.call-start = ((), (), s32[]{:S(2)}) async-start(), calls=%async_computation.6 | async-start | bytes 4669440 | tf_op jit(solution)/shard_map/all_gather | solution.py:146
  156.6 74.7 %all-gather.21.cloned.1.call-start = ((), (), s32[]{:S(2)}) async-start(), calls=%async_computation.12 | async-start | bytes 1327104 | tf_op jit(solution)/shard_map/all_gather | solution.py:159
  157.2 107.0 %all-gather.19.cloned.1.call-start = ((), (), s32[]{:S(2)}) async-start(), calls=%async_computation.11 | async-start | bytes 4669440 | tf_op jit(solution)/shard_map/all_gather | solution.py:163
  159.9 147.1 %all-gather.13.cloned.1.call-start = ((), (), s32[]{:S(2)}) async-start(), calls=%async_computation.7 | async-start | bytes 1327104 | tf_op jit(solution)/shard_map/all_gather | solution.py:122
  160.6 188.6 %all-gather.15.cloned.1.call-start = ((), (), s32[]{:S(2)}) async-start(), calls=%async_computation.8 | async-start | bytes 1327104 | tf_op jit(solution)/shard_map/all_gather | solution.py:123
  161.4 102.9 %copy-start.35 = (f32[768]{0:T(1024)S(1)}, f32[768]{0:T(1024)}, u32[]{:S(2)}) copy-start(f32[768]{0:T(1024)} %param.28) | copy-start | bytes 9220
  161.4 211.0 %reduce-scatter.9.cloned.1.call-start = ((), (), s32[]{:S(2)}) async-start(), calls=%async_computation.13 | async-start | bytes 4669440 | tf_op jit(solution)/shard_map/reduce_scatter | solution.py:167
  291.2 122.4 %reduce-scatter.7.cloned.1.call-start = ((), (), s32[]{:S(2)}) async-start(), calls=%async_computation.9 | async-start | bytes 4669440 | tf_op jit(solution)/shard_map/reduce_scatter | solution.py:149
  372.3 131.1 %all-gather.23.cloned.1.call-start = ((), (), s32[]{:S(2)}) async-start(), calls=%async_computation.14 | async-start | bytes 4669440 | tf_op jit(solution)/shard_map/all_gather | solution.py:176
  417.2 155.5 %reduce-scatter.11.cloned.1.call-start = ((), (), s32[]{:S(2)}) async-start(), calls=%async_computation.15 | async-start | bytes 4669440 | tf_op jit(solution)/shard_map/reduce_scatter | solution.py:184
  530.4 42.4 %copy-start.16 = (f32[2,297]{1,0:T(2,128)S(1)}, f32[2,297]{1,0:T(2,128)}, u32[]{:S(2)}) copy-start(f32[2,297]{1,0:T(2,128)} %copy-done.15) | copy-start | bytes 7132
  530.4 42.4 %copy-start.19 = (f32[768]{0:T(1024)S(1)}, f32[768]{0:T(1024)}, u32[]{:S(2)}) copy-start(f32[768]{0:T(1024)} %param.20) | copy-start | bytes 9220
  530.4 44.2 %copy-start.25 = (f32[2,297]{1,0:T(2,128)S(1)}, f32[2,297]{1,0:T(2,128)}, u32[]{:S(2)}) copy-start(f32[2,297]{1,0:T(2,128)} %copy-done.24) | copy-start | bytes 7132
  530.4 44.2 %copy-start.21 = (f32[2,297]{1,0:T(2,128)S(1)}, f32[2,297]{1,0:T(2,128)}, u32[]{:S(2)}) copy-start(f32[2,297]{1,0:T(2,128)} %copy-done.20) | copy-start | bytes 7132
  530.4 82.2 %all-reduce.3.cloned.1.call-start = ((), (), s32[]{:S(2)}) async-start(), calls=%async_computation.16 | async-start | bytes 638976 | tf_op jit(solution)/shard_map/psum | solution.py:189
  580.4 102.6 %all-reduce.5.cloned.1.call-start = ((), (), s32[]{:S(2)}) async-start(), calls=%async_computation.17 | async-start | bytes 638976 | tf_op jit(solution)/shard_map/psum | solution.py:189
  (31 other events, 266.9 us)
Sparse Core Ops, SparseCore 0:
  12.4 33.0 all-gather.8
  107.8 43.8 reduce-scatter.4
  291.3 41.6 reduce-scatter.8
  372.4 41.1 reduce-scatter.6
  580.5 32.1 all-reduce.2
Sparse Core Ops, SparseCore 1:
  110.6 42.7 all-gather.16
  156.7 31.7 all-gather.10
  190.8 40.5 all-gather.20
  233.0 31.2 all-gather.18
  266.4 40.5 all-gather.12
  309.2 40.0 all-gather.14
  417.3 31.7 all-gather.22
  530.5 42.2 reduce-scatter.10
  612.7 70.2 all-reduce.4
